TPU v7x, 128 devices: a whole 4x4x4 slice. The times are simulated.
128 devices in a mesh: rows: 64 (over y, z, x), cols: 2 (over core).
Axes of the slice: x: 4, y: 4, z: 4, core: 2. Of those that a mesh axis runs over, the one named last changes fastest.
Arguments:
- video: bfloat16 [512, 256, 256], P('rows', 'cols'), may hold values from -12 to 12
- foreground: float32 [512, 256, 256], P('rows', 'cols'), may hold values from -4 to 4
- scaled_dual: float32 [512, 256, 256], P('rows', 'cols'), may hold values from -2.5 to 2.5
Outputs:
- background: float32 [512, 256, 256], P('rows', 'cols')
- new_foreground: float32 [512, 256, 256], P('rows', 'cols')
- new_dual: float32 [512, 256, 256], P('rows', 'cols')
All inputs are finite; a program needn't handle non-finite values.
Results may differ from a plain program's by a relative error of at most 0.00035.
Values sent between devices are 32-bit elements; how exact they have to be, the bound alone decides.
A program may use at most 64 MiB of HBM per device.

v0:
```python
import jax
import jax.numpy as jnp
from jax import lax
from jax.sharding import PartitionSpec as P

K_ROOT = 8
K_SIGN = 6
K_TV = 8
threshold_ratio = 1.0
dual_step = 0.25
tv_weight = 1.0
HALO = K_TV


def shifted(x, axis, by):
    length = lax.axis_size(axis)
    pairs = [(i, i + by) for i in range(length) if 0 <= i + by < length]
    return lax.ppermute(x, axis, pairs)


def matmul(left, right):
    return jnp.dot(left, right, precision=lax.Precision.HIGHEST, preferred_element_type=jnp.float32)


def shrink_matrix(gram):
    size = gram.shape[0]
    identity = jnp.eye(size, dtype=jnp.float32)
    scale = jnp.sqrt(jnp.sum(gram * gram))
    root = gram / scale
    inverse = identity
    for sweep in range(K_ROOT):
        factor = 1.5 * identity - 0.5 * matmul(inverse, root)
        root = matmul(root, factor)
        inverse = matmul(factor, inverse)
    cutoff = threshold_ratio * jnp.trace(root) / size
    signed = root - cutoff * identity
    for sweep in range(K_SIGN):
        signed = 1.5 * signed - 0.5 * matmul(signed, matmul(signed, signed))
    return 0.5 * matmul(identity - cutoff * inverse, identity + signed)


def with_halo(pair):
    left = shifted(pair[:, :, -HALO:], "cols", 1)
    right = shifted(pair[:, :, :HALO], "cols", -1)
    pair = jnp.concatenate([left, pair, right], axis=2)
    up = shifted(pair[:, -HALO:], "rows", 1)
    down = shifted(pair[:, :HALO], "rows", -1)
    return jnp.concatenate([up, pair, down], axis=1)


def divergence(px, py):
    prev_x = jnp.concatenate([jnp.zeros_like(px[:1]), px[:-1]], axis=0)
    prev_y = jnp.concatenate([jnp.zeros_like(py[:, :1]), py[:, :-1]], axis=1)
    return prev_x - px + prev_y - py


def slopes(s):
    down = jnp.concatenate([s[1:] - s[:-1], jnp.zeros_like(s[:1])], axis=0)
    across = jnp.concatenate([s[:, 1:] - s[:, :-1], jnp.zeros_like(s[:, :1])], axis=1)
    return (down, across)


def per_device(video, foreground, scaled_dual):
    rows_here, cols_here, frames = foreground.shape
    total_rows = rows_here * lax.axis_size("rows")
    total_cols = cols_here * lax.axis_size("cols")
    observed = video.astype(jnp.float32)
    mixed = observed - foreground + scaled_dual
    a = observed + scaled_dual
    ext = with_halo(jnp.stack([a, mixed]))
    a_ext, mixed_ext = (ext[0], ext[1])
    flat = mixed.reshape(-1, frames)
    gram = lax.psum(matmul(flat.T, flat), ("rows", "cols"))
    shrink = shrink_matrix(gram)
    ext_rows, ext_cols = (rows_here + 2 * HALO, cols_here + 2 * HALO)
    background_ext = matmul(mixed_ext.reshape(-1, frames), shrink).reshape(
        ext_rows, ext_cols, frames
    )
    target = a_ext - background_ext
    first_row = lax.axis_index("rows") * rows_here - HALO
    first_col = lax.axis_index("cols") * cols_here - HALO
    g = first_row + lax.broadcasted_iota(jnp.int32, (ext_rows, 1, 1), 0)
    h = first_col + lax.broadcasted_iota(jnp.int32, (1, ext_cols, 1), 1)
    keep_x = (g >= 0) & (g <= total_rows - 2)
    keep_y = (h >= 0) & (h <= total_cols - 2)
    dual_x = jnp.zeros_like(target)
    dual_y = jnp.zeros_like(target)
    for sweep in range(K_TV):
        current = target - divergence(dual_x, dual_y)
        down, across = slopes(current)
        dual_x = jnp.where(keep_x, jnp.clip(dual_x + dual_step * down, -tv_weight, tv_weight), 0.0)
        dual_y = jnp.where(
            keep_y, jnp.clip(dual_y + dual_step * across, -tv_weight, tv_weight), 0.0
        )
    inner = (slice(HALO, HALO + rows_here), slice(HALO, HALO + cols_here))
    new_foreground = (target - divergence(dual_x, dual_y))[inner]
    background = background_ext[inner]
    new_dual = target[inner] - new_foreground
    return (background, new_foreground, new_dual)


def solution(mesh):
    return jax.shard_map(
        per_device,
        mesh=mesh,
        in_specs=(P("rows", "cols", None), P("rows", "cols", None), P("rows", "cols", None)),
        out_specs=(P("rows", "cols", None), P("rows", "cols", None), P("rows", "cols", None)),
        check_vma=False,
    )
```

profile of v0, /device:TPU:8, one launch (start us, length us, event | category | flops | bytes accessed | tf_op | source)
XLA Modules:
  0.0 341.0 jit_solution(16815311461451276916)
XLA Ops:
  7.2 5.3 %convolution_bitcast_fusion = f32[256,256]{1,0:T(8,128)} fusion(f32[8,128,256]{2,1,0:T(8,128)} %param.5, f32[8,128,256]{2,1,0:T(8,128)} %param.4, bf16[8,128,256]{2,1,0:T(8,128)(2,1)} %param.3), kind=kOutput, calls=%fused_computation.80 | convolution fusion | flops 806092800 | bytes 2883584 | tf_op jit(solution)/shard_map/dot_general | solution.py:22
  12.5 1.6 fusion.19
  14.2 1.7 collective-permute-start
  17.4 140.6 %all-reduce.34.cloned.1.call-done = f32[256,256]{1,0:T(8,128)} async-done(((f32[256,256]{1,0:T(8,128)}), f32[256,256]{1,0:T(8,128)}) %all-reduce.34.cloned.1.call-update) | async-done | bytes 262160 | tf_op jit(solution)/shard_map/psum | solution.py:73
  158.1 1.6 multiply_reduce_fusion
  173.7 5.3 %collective-permute-start.3 = (f32[2,8,144,256]{3,2,1,0:T(8,128)S(1)}, f32[2,8,144,256]{3,2,1,0:T(8,128)S(1)}, u32[]{:S(2)}, u32[]{:S(2)}) collective-permute-start(f32[2,8,144,256]{3,2,1,0:T(8,128)S(1)} %pad_maximum_fusion.1), channel_id=1, source_target_pairs={{2,0},{4,2},{6,4},{8,6},{10,8},{12,10},{14,12},{16,14},{18,16},{20... | collective-permute-start | bytes 7077896 | tf_op jit(solution)/shard_map/ppermute | solution.py:18
  179.0 2.1 collective-permute-start.2
  185.4 44.2 %collective-permute-done.3 = f32[2,8,144,256]{3,2,1,0:T(8,128)S(1)} collective-permute-done((f32[2,8,144,256]{3,2,1,0:T(8,128)S(1)}, f32[2,8,144,256]{3,2,1,0:T(8,128)S(1)}, u32[]{:S(2)}, u32[]{:S(2)}) %collective-permute-start.3) | collective-permute-done | bytes 2359328 | tf_op jit(solution)/shard_map/ppermute | solution.py:18
  229.6 8.3 %collective-permute-done.2 = f32[2,8,144,256]{3,2,1,0:T(8,128)S(1)} collective-permute-done((f32[2,8,144,256]{3,2,1,0:T(8,128)S(1)}, f32[2,8,144,256]{3,2,1,0:T(8,128)S(1)}, u32[]{:S(2)}, u32[]{:S(2)}) %collective-permute-start.2) | collective-permute-done | bytes 2359328 | tf_op jit(solution)/shard_map/ppermute | solution.py:18
  238.8 4.9 %fusion = (f32[24,144,256]{2,1,0:T(8,128)S(1)}, f32[24,144,256]{2,1,0:T(8,128)}) fusion(f32[2,24,144,256]{3,2,1,0:T(8,128)S(1)} %pad_maximum_fusion, f32[256,256,1]{1,0,2:T(8,128)S(1)} %fusion.2), kind=kOutput, calls=%fused_computation.10 | convolution fusion | flops 2718793728 | bytes 14417920 | tf_op jit(solution)/shard_map/dot_general | solution.py:22
  245.6 2.1 subtract_subtract_fusion.6
  248.5 2.3 clamp_select_fusion.12
  250.8 2.2 slice.233
  253.7 5.5 %subtract_subtract_fusion.5 = f32[24,144,256]{2,1,0:T(8,128)S(1)} fusion(f32[24,144,256]{2,1,0:T(8,128)S(1)} %get-tuple-element.11, f32[24,144,256]{2,1,0:T(8,128)S(1)} %get-tuple-element.13, f32[24,143,256]{2,1,0:T(8,128)S(1)} %bitcast.98, f32[24,144,256]{2,1,0:T(8,128)} %copy-done.16, f32[23,144,256]{2,1,0:T(8,128)} %slice.233), kind=kLoop, calls=%fused_computation.30 | loop fusion | flops 3538944 | bytes 21061632 | tf_op jit(solution)/shard_map/sub | solution.py:89
  259.9 1.5 copy-done.17
  265.2 2.0 slice.239
  267.2 4.9 %subtract_subtract_fusion.4 = f32[24,144,256]{2,1,0:T(8,128)S(1)} fusion(f32[24,144,256]{2,1,0:T(8,128)S(1)} %get-tuple-element.11, f32[24,144,256]{2,1,0:T(8,128)S(1)} %clamp_select_fusion.10, f32[24,143,256]{2,1,0:T(8,128)S(1)} %bitcast.94, f32[24,144,256]{2,1,0:T(8,128)} %copy-done.8, f32[23,144,256]{2,1,0:T(8,128)} %slice.239), kind=kLoop, calls=%fused_computation.27 | loop fusion | flops 3538944 | bytes 21061632 | tf_op jit(solution)/shard_map/sub | solution.py:89
  272.8 1.5 copy-done.9
  275.0 2.9 clamp_select_fusion.8
  278.0 2.0 slice.245
  281.2 4.9 %subtract_subtract_fusion.3 = f32[24,144,256]{2,1,0:T(8,128)S(1)} fusion(f32[24,144,256]{2,1,0:T(8,128)S(1)} %get-tuple-element.11, f32[24,144,256]{2,1,0:T(8,128)S(1)} %copy-done, f32[24,143,256]{2,1,0:T(8,128)S(1)} %bitcast.95, f32[24,144,256]{2,1,0:T(8,128)} %copy-done.10, f32[23,144,256]{2,1,0:T(8,128)} %slice.245), kind=kLoop, calls=%fused_computation.24 | loop fusion | flops 3538944 | bytes 21061632 | tf_op jit(solution)/shard_map/sub | solution.py:89
  286.8 1.5 copy-done.11
  289.2 2.9 clamp_select_fusion.6
  292.1 2.0 slice.251
  295.3 4.9 %subtract_subtract_fusion.2 = f32[24,144,256]{2,1,0:T(8,128)S(1)} fusion(f32[24,144,256]{2,1,0:T(8,128)S(1)} %get-tuple-element.11, f32[24,144,256]{2,1,0:T(8,128)S(1)} %copy-done.1, f32[24,143,256]{2,1,0:T(8,128)S(1)} %bitcast.96, f32[24,144,256]{2,1,0:T(8,128)} %copy-done.12, f32[23,144,256]{2,1,0:T(8,128)} %slice.251), kind=kLoop, calls=%fused_computation.21 | loop fusion | flops 3538944 | bytes 21061632 | tf_op jit(solution)/shard_map/sub | solution.py:89
  303.2 3.0 clamp_select_fusion.4
  306.2 2.0 slice.257
  309.4 4.9 %subtract_subtract_fusion.1 = f32[24,144,256]{2,1,0:T(8,128)S(1)} fusion(f32[24,144,256]{2,1,0:T(8,128)S(1)} %get-tuple-element.11, f32[24,144,256]{2,1,0:T(8,128)S(1)} %copy-done.2, f32[24,143,256]{2,1,0:T(8,128)S(1)} %bitcast.97, f32[24,144,256]{2,1,0:T(8,128)} %copy-done.14, f32[23,144,256]{2,1,0:T(8,128)} %slice.257), kind=kLoop, calls=%fused_computation.18 | loop fusion | flops 3538944 | bytes 21061632 | tf_op jit(solution)/shard_map/sub | solution.py:89
  320.4 2.0 slice.263
  322.4 4.9 %subtract_subtract_fusion = f32[24,144,256]{2,1,0:T(8,128)S(1)} fusion(f32[24,144,256]{2,1,0:T(8,128)S(1)} %get-tuple-element.11, f32[24,144,256]{2,1,0:T(8,128)S(1)} %clamp_select_fusion.2, f32[24,143,256]{2,1,0:T(8,128)S(1)} %bitcast.93, f32[24,144,256]{2,1,0:T(8,128)} %copy-done.6, f32[23,144,256]{2,1,0:T(8,128)} %slice.263), kind=kLoop, calls=%fused_computation.15 | loop fusion | flops 3538944 | bytes 21061632 | tf_op jit(solution)/shard_map/sub | solution.py:89
  328.0 2.5 slice.223
  332.2 1.8 slice_subtract_fusion.18
  (111 shorter events, 44.6 us)
Async XLA Ops:
  7.2 5.4 %copy-start.18 = (f32[8,128,256]{2,1,0:T(8,128)S(1)}, f32[8,128,256]{2,1,0:T(8,128)}, u32[]{:S(2)}) copy-start(f32[8,128,256]{2,1,0:T(8,128)} %param.5) | copy-start | bytes 3145732
  7.2 150.9 %all-reduce.34.cloned.1.call-start = ((), (), s32[]{:S(2)}) async-start(), calls=%async_computation | async-start | bytes 524288 | tf_op jit(solution)/shard_map/psum | solution.py:73
  14.2 159.3 %collective-permute-start = (f32[2,8,8,256]{3,2,1,0:T(8,128)S(1)}, f32[2,8,8,256]{3,2,1,0:T(8,128)S(1)}, u32[]{:S(2)}, u32[]{:S(2)}) collective-permute-start(f32[2,8,8,256]{3,2,1,0:T(8,128)S(1)} %get-tuple-element.5), channel_id=1, source_target_pairs={{0,1},{2,3},{4,5},{6,7},{8,9},{10,11},{12,13},{14,15},{16,17},{18,... | collective-permute-start | bytes 393224 | tf_op jit(solution)/shard_map/ppermute | solution.py:18
  15.9 157.6 %collective-permute-start.1 = (f32[2,8,8,256]{3,2,1,0:T(8,128)S(1)}, f32[2,8,8,256]{3,2,1,0:T(8,128)S(1)}, u32[]{:S(2)}, u32[]{:S(2)}) collective-permute-start(f32[2,8,8,256]{3,2,1,0:T(8,128)S(1)} %get-tuple-element.6), channel_id=1, source_target_pairs={{1,0},{3,2},{5,4},{7,6},{9,8},{11,10},{13,12},{15,14},{17,16},{19,... | collective-permute-start | bytes 393224 | tf_op jit(solution)/shard_map/ppermute | solution.py:18
  173.7 55.9 %collective-permute-start.3 = (f32[2,8,144,256]{3,2,1,0:T(8,128)S(1)}, f32[2,8,144,256]{3,2,1,0:T(8,128)S(1)}, u32[]{:S(2)}, u32[]{:S(2)}) collective-permute-start(f32[2,8,144,256]{3,2,1,0:T(8,128)S(1)} %pad_maximum_fusion.1), channel_id=1, source_target_pairs={{2,0},{4,2},{6,4},{8,6},{10,8},{12,10},{14,12},{16,14},{18,16},{20... | collective-permute-start | bytes 7077896 | tf_op jit(solution)/shard_map/ppermute | solution.py:18
  179.0 58.9 %collective-permute-start.2 = (f32[2,8,144,256]{3,2,1,0:T(8,128)S(1)}, f32[2,8,144,256]{3,2,1,0:T(8,128)S(1)}, u32[]{:S(2)}, u32[]{:S(2)}) collective-permute-start(f32[2,8,144,256]{3,2,1,0:T(8,128)S(1)} %pad_maximum_fusion.1), channel_id=1, source_target_pairs={{0,2},{2,4},{4,6},{6,8},{8,10},{10,12},{12,14},{14,16},{16,18},{18... | collective-permute-start | bytes 7077896 | tf_op jit(solution)/shard_map/ppermute | solution.py:18
  250.8 2.9 copy-start.16
  250.8 8.3 %copy-start.4 = (f32[24,144,256]{2,1,0:T(8,128)}, f32[24,144,256]{2,1,0:T(8,128)S(1)}, u32[]{:S(2)}) copy-start(f32[24,144,256]{2,1,0:T(8,128)S(1)} %get-tuple-element.13) | copy-start | bytes 10616836
  259.4 2.0 copy-start.17
  261.4 2.0 copy-start.5
  263.4 1.8 copy-start.8
  272.3 2.0 copy-start.9
  275.0 2.9 copy-start.10
  278.0 3.2 copy-start
  286.3 2.0 copy-start.11
  289.2 2.9 copy-start.12
  292.1 3.2 copy-start.1
  300.5 2.0 copy-start.13
  303.2 3.0 copy-start.14
  306.2 3.2 copy-start.2
  314.6 2.0 copy-start.15
  316.6 2.0 copy-start.3
  318.6 1.8 copy-start.6
  327.6 3.0 copy-start.7
Sparse Core Ops, SparseCore 0:
  13.3 144.7 all-reduce.33
where the time goes:
time: 344 us; the launch traced here: 341 us
  waiting for transfers between devices  193 us (56%)
  other arithmetic  62.3 us (18%)
  local copies, waits for them, and re-layouts  31.9 us (9%)
  matrix products  26.6 us (8%)
  between operations  16.3 us (5%)
  starting transfers between devices  10.7 us (3%)
    psum x1, waiting for transfers between devices, per_device(): gram = lax.psum(matmul(flat.T, flat), ('rows', 'cols'))  141 us
    ppermute x4, waiting for transfers between devices, shifted(): return lax.ppermute(x, axis, pairs)  52.5 us
    sub x7, other arithmetic, per_device(): current = target - divergence(dual_x, dual_y)  32.1 us
    dot_general x39, matrix products, matmul(): jnp.dot(left, right, precision=lax.Precision.HIGHEST, preferred_element_t...  26.6 us
    unnamed x38, local copies, waits for them, and re-layouts  16.6 us
    select_n x8, other arithmetic, per_device(): jnp.where(keep_y, jnp.clip(dual_y + dual_step * across, -tv_weight, tv_we...  13.8 us
    slice x8, local copies, waits for them, and re-layouts, divergence(): prev_x = jnp.concatenate([jnp.zeros_like(px[:1]), px[:-1]], axis=0)  12.7 us
    ppermute x4, starting transfers between devices, shifted(): return lax.ppermute(x, axis, pairs)  10.6 us
  transfers between devices with their start and end apart: 5, of which 3 were waited for; matrix products, arithmetic and copies ran while one was open for 6% of the time, Pallas kernels for 0%

commit v1 on v0

--- a/solution.py
+++ b/solution.py
@@ -70,7 +70,7 @@
     ext = with_halo(jnp.stack([a, mixed]))
     a_ext, mixed_ext = (ext[0], ext[1])
     flat = mixed.reshape(-1, frames)
-    gram = lax.psum(matmul(flat.T, flat), ("rows", "cols"))
+    gram = jnp.sum(lax.all_gather(matmul(flat.T, flat), ("rows", "cols")), axis=0)
     shrink = shrink_matrix(gram)
     ext_rows, ext_cols = (rows_here + 2 * HALO, cols_here + 2 * HALO)
     background_ext = matmul(mixed_ext.reshape(-1, frames), shrink).reshape(

time: 344 us -> 296 us (0.86)
  waiting for transfers between devices: 193 us -> 132 us
  other arithmetic: 62.3 us -> 74.2 us
    psum x1 -> x0, waiting for transfers between devices: 141 us -> none  [per_device(): gram = lax.psum(matmul(flat.T, flat), ('rows', 'cols'))]
    all_gather x0 -> x1, waiting for transfers between devices: none -> 77.7 us  [per_device(): lax.all_gather(matmul(flat.T, flat), ('rows', 'cols'))]
    reduce_sum x0 -> x1, other arithmetic: none -> 12.1 us  [per_device(): jnp.sum(lax.all_gather(matmul(flat.T, flat), ('rows', 'cols')), axis=0)]
    select_n x8, other arithmetic: 13.8 us -> 8.8 us  [per_device(): jnp.where(keep_y, jnp.clip(dual_y + dual_step * across, -tv_weight, tv_we...]
    concatenate x1, other arithmetic: 0.8 us -> 4.87 us  [with_halo(): return jnp.concatenate([up, pair, down], axis=1)]
    unnamed x38 -> x30, local copies, waits for them, and re-layouts: 16.6 us -> 14.3 us
  transfers between devices with their start and end apart: 5 -> 5, of which waited for: 3 -> 3; matrix products, arithmetic and copies ran while one was open for 6% -> 3% of each run, Pallas kernels for 0% -> 0%
where the time goes in v1:
time: 296 us; the launch traced here: 291 us
  waiting for transfers between devices  132 us (45%)
  other arithmetic  74.2 us (25%)
  local copies, waits for them, and re-layouts  29.5 us (10%)
  matrix products  25.6 us (9%)
  between operations  16.4 us (6%)
  starting transfers between devices  13.1 us (4%)
    all_gather x1, waiting for transfers between devices, per_device(): lax.all_gather(matmul(flat.T, flat), ('rows', 'cols'))  77.7 us
    ppermute x4, waiting for transfers between devices, shifted(): return lax.ppermute(x, axis, pairs)  54.6 us
    sub x7, other arithmetic, per_device(): current = target - divergence(dual_x, dual_y)  32.4 us
    dot_general x39, matrix products, matmul(): jnp.dot(left, right, precision=lax.Precision.HIGHEST, preferred_element_t...  25.6 us
    unnamed x30, local copies, waits for them, and re-layouts  14.3 us
    ppermute x4, starting transfers between devices, shifted(): return lax.ppermute(x, axis, pairs)  13.1 us
    slice x8, local copies, waits for them, and re-layouts, divergence(): prev_x = jnp.concatenate([jnp.zeros_like(px[:1]), px[:-1]], axis=0)  12.9 us
    reduce_sum x1, other arithmetic, per_device(): jnp.sum(lax.all_gather(matmul(flat.T, flat), ('rows', 'cols')), axis=0)  12.1 us
  transfers between devices with their start and end apart: 5, of which 3 were waited for; matrix products, arithmetic and copies ran while one was open for 3% of the time, Pallas kernels for 0%

profile of v1, /device:TPU:8, one launch (start us, length us, event | category | flops | bytes accessed | tf_op | source)
XLA Modules:
  0.0 291.1 jit_solution(12433850203861000537)
XLA Ops:
  7.2 5.2 %convolution_bitcast_fusion = f32[256,256]{1,0:T(8,128)} fusion(f32[8,128,256]{2,1,0:T(8,128)} %param.5, f32[8,128,256]{2,1,0:T(8,128)} %param.4, bf16[8,128,256]{2,1,0:T(8,128)(2,1)} %param.3), kind=kOutput, calls=%fused_computation.80 | convolution fusion | flops 806092800 | bytes 2883584 | tf_op jit(solution)/shard_map/dot_general | solution.py:22
  12.4 1.6 fusion.19
  14.0 1.7 collective-permute-start
  17.1 1.9 collective-permute-done.1
  19.0 1.6 pad_maximum_fusion.1
  20.6 3.4 %collective-permute-start.2 = (f32[2,8,144,256]{3,2,1,0:T(8,128)}, f32[2,8,144,256]{3,2,1,0:T(8,128)}, u32[]{:S(2)}, u32[]{:S(2)}) collective-permute-start(f32[2,8,144,256]{3,2,1,0:T(8,128)} %pad_maximum_fusion.1), channel_id=1, source_target_pairs={{0,2},{2,4},{4,6},{6,8},{8,10},{10,12},{12,14},{14,16},{16,18},{18... | collective-permute-start | bytes 7077896 | tf_op jit(solution)/shard_map/ppermute | solution.py:18
  24.0 6.7 %collective-permute-start.3 = (f32[2,8,144,256]{3,2,1,0:T(8,128)}, f32[2,8,144,256]{3,2,1,0:T(8,128)}, u32[]{:S(2)}, u32[]{:S(2)}) collective-permute-start(f32[2,8,144,256]{3,2,1,0:T(8,128)} %pad_maximum_fusion.1), channel_id=1, source_target_pairs={{2,0},{4,2},{6,4},{8,6},{10,8},{12,10},{14,12},{16,14},{18,16},{20... | collective-permute-start | bytes 7077896 | tf_op jit(solution)/shard_map/ppermute | solution.py:18
  30.7 52.6 %collective-permute-done.2 = f32[2,8,144,256]{3,2,1,0:T(8,128)} collective-permute-done((f32[2,8,144,256]{3,2,1,0:T(8,128)}, f32[2,8,144,256]{3,2,1,0:T(8,128)}, u32[]{:S(2)}, u32[]{:S(2)}) %collective-permute-start.2) | collective-permute-done | bytes 2359328 | tf_op jit(solution)/shard_map/ppermute | solution.py:18
  83.4 4.9 %pad_maximum_fusion = f32[2,24,144,256]{3,2,1,0:T(8,128)} fusion(f32[2,8,144,256]{3,2,1,0:T(8,128)} %collective-permute-done.3, f32[2,8,8,256]{3,2,1,0:T(8,128)S(1)} %collective-permute-done.1, f32[1,8,128,256]{3,2,1,0:T(8,128)S(1)} %get-tuple-element.8, f32[1,8,128,256]{3,2,1,0:T(8,128)S(1)} %get-tuple-element.7, ...), kind=kLoop, calls=%fused_computation | loop fusion | flops 8847360 | bytes 14155776 | tf_op jit(solution)/shard_map/concatenate | solution.py:48
  88.2 77.7 %all-gather.3.cloned.1.call-done = f32[32768,256]{1,0:T(8,128)} async-done(((f32[256,256]{1,0:T(8,128)}), f32[32768,256]{1,0:T(8,128)}) %all-gather.3.cloned.1.call-update) | async-done | bytes 33554448 | tf_op jit(solution)/shard_map/all_gather | solution.py:73
  166.0 12.1 %reduce_sum.28 = f32[256,256]{1,0:T(8,128)S(1)} reduce(f32[128,256,256]{2,1,0:T(8,128)} %bitcast.100, f32[]{:T(128)} %constant.16.clone.1), dimensions={0}, to_apply=%region_0.0 | reduce | flops 8323072 | bytes 33816580 | tf_op jit(solution)/shard_map/reduce_sum | solution.py:73
  196.2 4.7 %fusion = (f32[24,144,256]{2,1,0:T(8,128)S(1)}, f32[24,144,256]{2,1,0:T(8,128)}) fusion(f32[2,24,144,256]{3,2,1,0:T(8,128)S(1)} %bitcast.103, f32[256,256,1]{1,0,2:T(8,128)S(1)} %fusion.2), kind=kOutput, calls=%fused_computation.10 | convolution fusion | flops 2718793728 | bytes 14417920 | tf_op jit(solution)/shard_map/dot_general | solution.py:22
  202.9 2.1 subtract_subtract_fusion.6
  205.8 2.2 clamp_select_fusion.12
  208.0 2.2 slice.233
  210.9 4.9 %subtract_subtract_fusion.5 = f32[24,144,256]{2,1,0:T(8,128)S(1)} fusion(f32[24,144,256]{2,1,0:T(8,128)S(1)} %get-tuple-element.11, f32[24,144,256]{2,1,0:T(8,128)S(1)} %get-tuple-element.13, f32[24,143,256]{2,1,0:T(8,128)S(1)} %bitcast.99, f32[24,144,256]{2,1,0:T(8,128)} %copy-done.9, f32[23,144,256]{2,1,0:T(8,128)} %slice.233), kind=kLoop, calls=%fused_computation.30 | loop fusion | flops 3538944 | bytes 21061632 | tf_op jit(solution)/shard_map/sub | solution.py:89
  218.7 2.2 slice.239
  221.6 4.9 %subtract_subtract_fusion.4 = f32[24,144,256]{2,1,0:T(8,128)S(1)} fusion(f32[24,144,256]{2,1,0:T(8,128)S(1)} %get-tuple-element.11, f32[24,144,256]{2,1,0:T(8,128)S(1)} %clamp_select_fusion.10, f32[24,143,256]{2,1,0:T(8,128)S(1)} %bitcast.95, f32[24,144,256]{2,1,0:T(8,128)} %copy-done.3, f32[23,144,256]{2,1,0:T(8,128)} %slice.239), kind=kLoop, calls=%fused_computation.27 | loop fusion | flops 3538944 | bytes 21061632 | tf_op jit(solution)/shard_map/sub | solution.py:89
  229.5 1.8 copy-done.5
  231.3 2.0 slice.245
  234.0 4.9 %subtract_subtract_fusion.3 = f32[24,144,256]{2,1,0:T(8,128)S(1)} fusion(f32[24,144,256]{2,1,0:T(8,128)S(1)} %get-tuple-element.11, f32[24,144,256]{2,1,0:T(8,128)S(1)} %clamp_select_fusion.8, f32[24,143,256]{2,1,0:T(8,128)S(1)} %bitcast.96, f32[24,144,256]{2,1,0:T(8,128)} %copy-done.5, f32[23,144,256]{2,1,0:T(8,128)} %slice.245), kind=kLoop, calls=%fused_computation.24 | loop fusion | flops 3538944 | bytes 21061632 | tf_op jit(solution)/shard_map/sub | solution.py:89
  242.0 2.0 slice.251
  244.0 2.5 clamp_select_fusion.6
  246.5 5.8 %subtract_subtract_fusion.2 = f32[24,144,256]{2,1,0:T(8,128)S(1)} fusion(f32[24,144,256]{2,1,0:T(8,128)S(1)} %get-tuple-element.11, f32[24,144,256]{2,1,0:T(8,128)} %clamp_select_fusion.6, f32[24,143,256]{2,1,0:T(8,128)} %bitcast.97, f32[24,144,256]{2,1,0:T(8,128)S(1)} %clamp_select_fusion.7, f32[23,144,256]{2,1,0:T(8,128)} %slice.251), kind=kLoop, calls=%fused_computation.21 | loop fusion | flops 3538944 | bytes 21061632 | tf_op jit(solution)/shard_map/sub | solution.py:89
  253.7 2.0 slice.257
  255.8 2.5 copy-done
  258.9 4.9 %subtract_subtract_fusion.1 = f32[24,144,256]{2,1,0:T(8,128)S(1)} fusion(f32[24,144,256]{2,1,0:T(8,128)S(1)} %get-tuple-element.11, f32[24,144,256]{2,1,0:T(8,128)S(1)} %clamp_select_fusion.4, f32[24,143,256]{2,1,0:T(8,128)S(1)} %bitcast.98, f32[24,144,256]{2,1,0:T(8,128)} %copy-done.7, f32[23,144,256]{2,1,0:T(8,128)} %slice.257), kind=kLoop, calls=%fused_computation.18 | loop fusion | flops 3538944 | bytes 21061632 | tf_op jit(solution)/shard_map/sub | solution.py:89
  266.8 1.8 copy-done.1
  268.6 2.0 slice.263
  271.3 4.9 %subtract_subtract_fusion = f32[24,144,256]{2,1,0:T(8,128)S(1)} fusion(f32[24,144,256]{2,1,0:T(8,128)S(1)} %get-tuple-element.11, f32[24,144,256]{2,1,0:T(8,128)S(1)} %clamp_select_fusion.2, f32[24,143,256]{2,1,0:T(8,128)S(1)} %bitcast.94, f32[24,144,256]{2,1,0:T(8,128)} %copy-done.1, f32[23,144,256]{2,1,0:T(8,128)} %slice.263), kind=kLoop, calls=%fused_computation.15 | loop fusion | flops 3538944 | bytes 21061632 | tf_op jit(solution)/shard_map/sub | solution.py:89
  280.1 2.3 slice.223
  282.4 1.7 slice_subtract_fusion.18
  (105 shorter events, 41.0 us)
Async XLA Ops:
  7.2 5.2 %copy-start.11 = (f32[8,128,256]{2,1,0:T(8,128)S(1)}, f32[8,128,256]{2,1,0:T(8,128)}, u32[]{:S(2)}) copy-start(f32[8,128,256]{2,1,0:T(8,128)} %param.5) | copy-start | bytes 3145732
  7.2 158.8 %all-gather.3.cloned.1.call-start = ((), (), s32[]{:S(2)}) async-start(), calls=%async_computation | async-start | bytes 33816576 | tf_op jit(solution)/shard_map/all_gather | solution.py:73
  14.0 3.1 %collective-permute-start = (f32[2,8,8,256]{3,2,1,0:T(8,128)S(1)}, f32[2,8,8,256]{3,2,1,0:T(8,128)S(1)}, u32[]{:S(2)}, u32[]{:S(2)}) collective-permute-start(f32[2,8,8,256]{3,2,1,0:T(8,128)S(1)} %get-tuple-element.5), channel_id=1, source_target_pairs={{0,1},{2,3},{4,5},{6,7},{8,9},{10,11},{12,13},{14,15},{16,17},{18,... | collective-permute-start | bytes 393224 | tf_op jit(solution)/shard_map/ppermute | solution.py:18
  15.8 3.2 %collective-permute-start.1 = (f32[2,8,8,256]{3,2,1,0:T(8,128)S(1)}, f32[2,8,8,256]{3,2,1,0:T(8,128)S(1)}, u32[]{:S(2)}, u32[]{:S(2)}) collective-permute-start(f32[2,8,8,256]{3,2,1,0:T(8,128)S(1)} %get-tuple-element.6), channel_id=1, source_target_pairs={{1,0},{3,2},{5,4},{7,6},{9,8},{11,10},{13,12},{15,14},{17,16},{19,... | collective-permute-start | bytes 393224 | tf_op jit(solution)/shard_map/ppermute | solution.py:18
  20.6 62.7 %collective-permute-start.2 = (f32[2,8,144,256]{3,2,1,0:T(8,128)}, f32[2,8,144,256]{3,2,1,0:T(8,128)}, u32[]{:S(2)}, u32[]{:S(2)}) collective-permute-start(f32[2,8,144,256]{3,2,1,0:T(8,128)} %pad_maximum_fusion.1), channel_id=1, source_target_pairs={{0,2},{2,4},{4,6},{6,8},{8,10},{10,12},{12,14},{14,16},{16,18},{18... | collective-permute-start | bytes 7077896 | tf_op jit(solution)/shard_map/ppermute | solution.py:18
  24.0 59.3 %collective-permute-start.3 = (f32[2,8,144,256]{3,2,1,0:T(8,128)}, f32[2,8,144,256]{3,2,1,0:T(8,128)}, u32[]{:S(2)}, u32[]{:S(2)}) collective-permute-start(f32[2,8,144,256]{3,2,1,0:T(8,128)} %pad_maximum_fusion.1), channel_id=1, source_target_pairs={{2,0},{4,2},{6,4},{8,6},{10,8},{12,10},{14,12},{16,14},{18,16},{20... | collective-permute-start | bytes 7077896 | tf_op jit(solution)/shard_map/ppermute | solution.py:18
  186.3 9.9 %slice-start = ((s8[7077888]{0:T(1024)(128)(4,1)}), s8[2883584]{0:T(1024)(128)(4,1)S(1)}, s32[]{:S(2)}) async-start(s8[7077888]{0:T(1024)(128)(4,1)} %bitcast.102), calls=%async_computation.1 | async-start | bytes 5767168
  187.8 1.0 copy-start.12
  192.0 4.1 %slice-start.1 = ((s8[7077888]{0:T(1024)(128)(4,1)}), s8[4194304]{0:T(1024)(128)(4,1)S(1)}, s32[]{:S(2)}) async-start(s8[7077888]{0:T(1024)(128)(4,1)} %bitcast.102), calls=%async_computation.2 | async-start | bytes 8388608
  208.0 2.9 copy-start.9
  216.0 2.0 copy-start.10
  218.7 2.9 copy-start.3
  226.8 2.0 copy-start.4
  229.5 1.8 copy-start.5
  239.1 2.0 copy-start.6
  253.7 5.2 %copy-start.7 = (f32[24,144,256]{2,1,0:T(8,128)}, f32[24,144,256]{2,1,0:T(8,128)S(1)}, u32[]{:S(2)}) copy-start(f32[24,144,256]{2,1,0:T(8,128)S(1)} %clamp_select_fusion.5) | copy-start | bytes 10616836
  253.7 4.5 %copy-start = (f32[24,144,256]{2,1,0:T(8,128)S(1)}, f32[24,144,256]{2,1,0:T(8,128)}, u32[]{:S(2)}) copy-start(f32[24,144,256]{2,1,0:T(8,128)} %clamp_select_fusion.6) | copy-start | bytes 10616836
  264.1 2.0 copy-start.8
  266.8 1.8 copy-start.1
  276.5 2.0 copy-start.2
Sparse Core Ops, SparseCore 0:
  12.5 153.3 all-gather.2
